TPU v7x, 32 devices: a whole 2x2x4 slice. The times are simulated.
32 devices in a mesh: fsdp: 4 (over y, x), ctx: 8 (over z, core).
Axes of the slice: x: 2, y: 2, z: 4, core: 2. Of those that a mesh axis runs over, the one named last changes fastest.
Arguments:
- block_input: bfloat16 [8, 512, 1088], P('fsdp', 'ctx'), may hold values from -6 to 6
- positions: int32 [8, 512], P('fsdp', 'ctx'), may hold values from 0 to 511, as said below
- prefix: int32 [8], P('fsdp'), may hold values from 0 to 255
- first_gain: float32 [1088], replicated, may hold values from 0.25 to 1.75
- first_bias: float32 [1088], replicated, may hold values from -3 to 3
- query_key_value: bfloat16 [1088, 3264], P('fsdp')
- query_value_bias: float32 [2, 1088], replicated, may hold values from -3 to 3
- output_weight: bfloat16 [1088, 1088], P('fsdp'), may hold values from -1.5 to 1.5
- output_bias: float32 [1088], replicated, may hold values from -3 to 3
- second_gain: float32 [1088], replicated, may hold values from 0.25 to 1.75
- second_bias: float32 [1088], replicated, may hold values from -3 to 3
- expand_weight: bfloat16 [1088, 4352], P('fsdp'), may hold values from -0.1875 to 0.1875
- expand_bias: float32 [4352], replicated, may hold values from -3 to 3
- contract_weight: bfloat16 [4352, 1088], P('fsdp'), may hold values from -0.09375 to 0.09375
- contract_bias: float32 [1088], replicated, may hold values from -3 to 3
- cotangent: bfloat16 [8, 512, 1088], P('fsdp', 'ctx'), may hold values from -6 to 6
Outputs:
- block_output: bfloat16 [8, 512, 1088], P('fsdp', 'ctx')
- input_gradient: float32 [8, 512, 1088], P('fsdp', 'ctx')
- first_gain_gradient: float32 [1088], replicated
- first_bias_gradient: float32 [1088], replicated
- query_key_value_gradient: float32 [1088, 3264], P('fsdp')
- query_value_bias_gradient: float32 [2, 1088], replicated
- output_weight_gradient: float32 [1088, 1088], P('fsdp')
- output_bias_gradient: float32 [1088], replicated
- second_gain_gradient: float32 [1088], replicated
- second_bias_gradient: float32 [1088], replicated
- expand_weight_gradient: float32 [1088, 4352], P('fsdp')
- expand_bias_gradient: float32 [4352], replicated
- contract_weight_gradient: float32 [4352, 1088], P('fsdp')
- contract_bias_gradient: float32 [1088], replicated
Inputs may be any that keep to these rules, and one draw needn't show every extreme that they name: Each row lists the positions 0 to 511 once, as blocks of 64 consecutive increasing positions whose order along the row is arbitrary; a device's tokens of a sequence form one such block.
All inputs are finite; a program needn't handle non-finite values.
Results may differ from a plain program's by a relative error of at most 0.017.
Values may be sent and summed in bfloat16 or wider, within the bound.
No kernel may reach another device: no remote copies, remote signals or barrier semaphores. Data moves between devices by JAX's collectives and lax.ppermute only.
A program may use at most 256 MiB of HBM per device.

v0:
```python
import jax
import jax.numpy as jnp
from jax import lax
from jax.sharding import PartitionSpec as P

HEAD_DIM = 64
EPSILON = 1e-05
NEGATIVE = -1e30


def layer_norm(values, gain, bias):
    center = values - jnp.mean(values, axis=-1, keepdims=True)
    inverse = lax.rsqrt(jnp.mean(center * center, axis=-1, keepdims=True) + EPSILON)
    normed = center * inverse
    return (normed * gain + bias, normed, inverse)


def norm_back(upper, normed, inverse, gain):
    scaled = upper * gain
    return inverse * (
        scaled
        - jnp.mean(scaled, axis=-1, keepdims=True)
        - normed * jnp.mean(scaled * normed, axis=-1, keepdims=True)
    )


def gelu(values):
    return jax.nn.gelu(values, approximate=True)


def term_of(left, right):
    return jnp.einsum("ti,tj->ij", left, right, preferred_element_type=jnp.float32)


def per_device(
    block_input,
    positions,
    prefix,
    first_gain,
    first_bias,
    query_key_value,
    query_value_bias,
    output_weight,
    output_bias,
    second_gain,
    second_bias,
    expand_weight,
    expand_bias,
    contract_weight,
    contract_bias,
    cotangent,
):
    sequences, piece, width = block_input.shape
    heads = width // HEAD_DIM
    scale = HEAD_DIM ** (-0.5)
    rows = sequences * piece
    joint_full, output_full, expand_full, contract_full = (
        lax.all_gather(query_key_value, "fsdp", axis=0, tiled=True),
        lax.all_gather(output_weight, "fsdp", axis=0, tiled=True),
        lax.all_gather(expand_weight, "fsdp", axis=0, tiled=True),
        lax.all_gather(contract_weight, "fsdp", axis=0, tiled=True),
    )
    all_places = lax.all_gather(positions, "ctx", axis=1, tiled=True)
    limits = jnp.maximum(positions, prefix[:, None] - 1)
    input_rows = block_input.reshape(rows, width).astype(jnp.float32)
    first_out, first_normed, first_inverse = layer_norm(input_rows, first_gain, first_bias)
    first_round = first_out.astype(jnp.bfloat16)
    joint = jnp.dot(first_round, joint_full, preferred_element_type=jnp.float32)
    query = (joint[:, :width] + query_value_bias[0]).astype(jnp.bfloat16)
    keys = joint[:, width : 2 * width].astype(jnp.bfloat16)
    values = (joint[:, 2 * width :] + query_value_bias[1]).astype(jnp.bfloat16)
    query_heads = query.reshape(sequences, piece, heads, HEAD_DIM)
    key_rows = keys.reshape(sequences, piece, width)
    value_rows = values.reshape(sequences, piece, width)
    key_piece = lax.all_gather(key_rows, "ctx", axis=1, tiled=True)
    top = jnp.full((sequences, heads, piece), NEGATIVE, jnp.float32)
    count = key_piece.shape[1]
    fold_key_heads = key_piece.reshape(sequences, count, heads, HEAD_DIM)
    scores = (
        jnp.einsum(
            "bqhd,bkhd->bhqk", query_heads, fold_key_heads, preferred_element_type=jnp.float32
        )
        * scale
    )
    visible = all_places[:, None, None, :] <= limits[:, None, :, None]
    new_top = jnp.maximum(top, jnp.max(jnp.where(visible, scores, NEGATIVE), axis=-1))
    weights = jnp.where(visible, jnp.exp(scores - new_top[..., None]), 0.0)
    total = jnp.sum(weights, axis=-1)
    top, total = (new_top, total)
    log_heads = top + jnp.log(total)

    def fold_keys(pieces):
        key_piece, value_piece = pieces
        count = key_piece.shape[1]
        key_heads = key_piece.reshape(sequences, count, heads, HEAD_DIM)
        value_heads = value_piece.reshape(sequences, count, heads, HEAD_DIM)
        scores = (
            jnp.einsum(
                "bqhd,bkhd->bhqk", query_heads, key_heads, preferred_element_type=jnp.float32
            )
            * scale
        )
        visible = all_places[:, None, None, :] <= limits[:, None, :, None]
        shares = jnp.where(visible, jnp.exp(scores - log_heads[..., None]), 0.0).astype(
            jnp.bfloat16
        )
        return jnp.einsum(
            "bhqk,bkhd->bqhd", shares, value_heads, preferred_element_type=jnp.float32
        )

    summed = fold_keys(
        (
            lax.all_gather(key_rows, "ctx", axis=1, tiled=True),
            lax.all_gather(value_rows, "ctx", axis=1, tiled=True),
        )
    )
    mixed = summed.astype(jnp.bfloat16).reshape(rows, width)
    log_total = jnp.swapaxes(log_heads, 1, 2)
    residual = (
        input_rows + jnp.dot(mixed, output_full, preferred_element_type=jnp.float32) + output_bias
    )
    second_out, second_normed, second_inverse = layer_norm(residual, second_gain, second_bias)
    second_round = second_out.astype(jnp.bfloat16)
    before = jnp.dot(second_round, expand_full, preferred_element_type=jnp.float32) + expand_bias
    after, gelu_back = jax.vjp(gelu, before)
    after_round = after.astype(jnp.bfloat16)
    block_output = (
        (
            residual
            + jnp.dot(after_round, contract_full, preferred_element_type=jnp.float32)
            + contract_bias
        )
        .astype(jnp.bfloat16)
        .reshape(sequences, piece, width)
    )
    joint_full, output_full, expand_full, contract_full = (
        lax.all_gather(query_key_value, "fsdp", axis=0, tiled=True),
        lax.all_gather(output_weight, "fsdp", axis=0, tiled=True),
        lax.all_gather(expand_weight, "fsdp", axis=0, tiled=True),
        lax.all_gather(contract_weight, "fsdp", axis=0, tiled=True),
    )
    upper = cotangent.reshape(rows, width)
    upper_wide = upper.astype(jnp.float32)
    after_grad = jnp.dot(upper, contract_full.T, preferred_element_type=jnp.float32)
    before_grad = gelu_back(after_grad)[0]
    before_round = before_grad.astype(jnp.bfloat16)
    second_grad = jnp.dot(before_round, expand_full.T, preferred_element_type=jnp.float32)
    residual_grad = upper_wide + norm_back(second_grad, second_normed, second_inverse, second_gain)
    residual_round = residual_grad.astype(jnp.bfloat16)
    mixed_grad = jnp.dot(residual_round, output_full.T, preferred_element_type=jnp.float32).astype(
        jnp.bfloat16
    )
    flows = jnp.sum(
        (mixed_grad.astype(jnp.float32) * mixed.astype(jnp.float32)).reshape(
            sequences, piece, heads, HEAD_DIM
        ),
        axis=-1,
    )
    all_query, all_upper = (
        lax.all_gather(query.reshape(sequences, piece, width), "ctx", axis=1, tiled=True),
        lax.all_gather(mixed_grad.reshape(sequences, piece, width), "ctx", axis=1, tiled=True),
    )
    all_log, all_flows = (
        lax.all_gather(log_total, "ctx", axis=1, tiled=True),
        lax.all_gather(flows, "ctx", axis=1, tiled=True),
    )
    all_limits = jnp.maximum(all_places, prefix[:, None] - 1)
    length = all_query.shape[1]
    span = min(512, length)
    key_heads = keys.reshape(sequences, piece, heads, HEAD_DIM)
    value_heads = values.reshape(sequences, piece, heads, HEAD_DIM)

    def back_block(number, state):
        key_grad, value_grad, terms = state
        start = number * span
        part = lax.dynamic_slice_in_dim(all_query, start, span, 1).reshape(
            sequences, span, heads, HEAD_DIM
        )
        above = lax.dynamic_slice_in_dim(all_upper, start, span, 1).reshape(
            sequences, span, heads, HEAD_DIM
        )
        log_part = lax.dynamic_slice_in_dim(all_log, start, span, 1)
        flow_part = lax.dynamic_slice_in_dim(all_flows, start, span, 1)
        limit = lax.dynamic_slice_in_dim(all_limits, start, span, 1)
        scores = (
            jnp.einsum("bqhd,bkhd->bhqk", part, key_heads, preferred_element_type=jnp.float32)
            * scale
        )
        visible = positions[:, None, None, :] <= limit[:, None, :, None]
        shares = jnp.where(visible, jnp.exp(scores - jnp.swapaxes(log_part, 1, 2)[..., None]), 0.0)
        share_grad = jnp.einsum(
            "bqhd,bkhd->bhqk", above, value_heads, preferred_element_type=jnp.float32
        )
        score_grad = shares * (share_grad - jnp.swapaxes(flow_part, 1, 2)[..., None])
        score_round = score_grad.astype(jnp.bfloat16)
        key_grad = (
            key_grad
            + jnp.einsum("bhqk,bqhd->bkhd", score_round, part, preferred_element_type=jnp.float32)
            * scale
        )
        value_grad = value_grad + jnp.einsum(
            "bhqk,bqhd->bkhd",
            shares.astype(jnp.bfloat16),
            above,
            preferred_element_type=jnp.float32,
        )
        query_grad = (
            jnp.einsum(
                "bhqk,bkhd->bqhd", score_round, key_heads, preferred_element_type=jnp.float32
            )
            * scale
        )
        terms = lax.dynamic_update_slice_in_dim(
            terms, query_grad.reshape(sequences, span, width), start, 1
        )
        return (key_grad, value_grad, terms)

    zero_heads = jnp.zeros((sequences, piece, heads, HEAD_DIM), jnp.float32)
    empty_terms = jnp.zeros((sequences, length, width), jnp.float32)
    key_grad, value_grad, terms = lax.fori_loop(
        0, length // span, back_block, (zero_heads, zero_heads, empty_terms)
    )
    query_grad = lax.psum_scatter(terms, "ctx", scatter_dimension=1, tiled=True).reshape(
        rows, width
    )
    key_grad = key_grad.reshape(rows, width)
    value_grad = value_grad.reshape(rows, width)
    joint_grad = jnp.concatenate([query_grad, key_grad, value_grad], axis=1).astype(jnp.bfloat16)
    first_grad = jnp.dot(joint_grad, joint_full.T, preferred_element_type=jnp.float32)
    input_gradient = (
        residual_grad + norm_back(first_grad, first_normed, first_inverse, first_gain)
    ).reshape(sequences, piece, width)
    joint_share = lax.psum_scatter(
        term_of(first_round, joint_grad), "fsdp", scatter_dimension=0, tiled=True
    )
    output_share = lax.psum_scatter(
        term_of(mixed, residual_round), "fsdp", scatter_dimension=0, tiled=True
    )
    expand_share = lax.psum_scatter(
        term_of(second_round, before_round), "fsdp", scatter_dimension=0, tiled=True
    )
    contract_share = lax.psum_scatter(
        term_of(after_round, upper), "fsdp", scatter_dimension=0, tiled=True
    )
    joint_sum, output_sum, expand_sum, contract_sum = lax.psum(
        (joint_share, output_share, expand_share, contract_share), "ctx"
    )
    small = lax.psum(
        (
            jnp.sum(first_grad * first_normed, axis=0),
            jnp.sum(first_grad, axis=0),
            jnp.stack([jnp.sum(query_grad, axis=0), jnp.sum(value_grad, axis=0)]),
            jnp.sum(residual_grad, axis=0),
            jnp.sum(second_grad * second_normed, axis=0),
            jnp.sum(second_grad, axis=0),
            jnp.sum(before_grad, axis=0),
            jnp.sum(upper_wide, axis=0),
        ),
        ("fsdp", "ctx"),
    )
    return (
        block_output,
        input_gradient,
        small[0],
        small[1],
        joint_sum,
        small[2],
        output_sum,
        small[3],
        small[4],
        small[5],
        expand_sum,
        small[6],
        contract_sum,
        small[7],
    )


def solution(mesh):
    in_specs = (
        P("fsdp", "ctx", None),
        P("fsdp", "ctx"),
        P("fsdp"),
        P(),
        P(),
        P("fsdp", None),
        P(),
        P("fsdp", None),
        P(),
        P(),
        P(),
        P("fsdp", None),
        P(),
        P("fsdp", None),
        P(),
        P("fsdp", "ctx", None),
    )
    out_specs = (
        P("fsdp", "ctx", None),
        P("fsdp", "ctx", None),
        P(),
        P(),
        P("fsdp", None),
        P(),
        P("fsdp", None),
        P(),
        P(),
        P(),
        P("fsdp", None),
        P(),
        P("fsdp", None),
        P(),
    )
    return jax.shard_map(
        per_device, mesh=mesh, in_specs=in_specs, out_specs=out_specs, check_vma=False
    )
```

profile of v0, /device:TPU:0, one launch (start us, length us, event | category | flops | bytes accessed | tf_op | source)
XLA Modules:
  0.0 1415.7 jit_solution(14344551594454998313)
XLA Ops:
  9.5 81.1 %all-gather.10.cloned.1.call-done = bf16[1088,3264]{1,0:T(8,128)(2,1)} async-done(((bf16[272,3264]{1,0:T(8,128)(2,1)}), bf16[1088,3264]{1,0:T(8,128)(2,1)}) %all-gather.10.cloned.1.call-update) | async-done | bytes 7102480 | tf_op jit(solution)/shard_map/all_gather | solution.py:58
  90.5 6.3 fusion.48
  100.5 11.7 all-gather
  114.6 78.9 %all-gather.20.cloned.1.call-done = bf16[4352,1088]{1,0:T(8,128)(2,1)} async-done(((bf16[1088,1088]{1,0:T(8,128)(2,1)}), bf16[4352,1088]{1,0:T(8,128)(2,1)}) %all-gather.20.cloned.1.call-update) | async-done | bytes 9469968 | tf_op jit(solution)/shard_map/all_gather | solution.py:61
  193.5 8.0 fusion.56
  201.5 25.7 %all-gather.14.cloned.1.call-done = bf16[2,512,1088]{2,1,0:T(8,128)(2,1)} async-done(((bf16[2,64,1088]{2,1,0:T(8,128)(2,1)}), bf16[2,512,1088]{2,1,0:T(8,128)(2,1)}) %all-gather.14.cloned.1.call-update) | async-done | bytes 2228240 | tf_op jit(solution)/shard_map/all_gather | solution.py:113
  233.2 26.7 %all-gather.12.cloned.1.call-done = bf16[2,512,1088]{2,1,0:T(8,128)(2,1)} async-done(((bf16[2,64,1088]{2,1,0:T(8,128)(2,1)}), bf16[2,512,1088]{2,1,0:T(8,128)(2,1)}) %all-gather.12.cloned.1.call-update) | async-done | bytes 2228240 | tf_op jit(solution)/shard_map/all_gather | solution.py:114
  267.5 31.9 %all-gather.16.cloned.1.call-done = bf16[1088,1088]{1,0:T(8,128)(2,1)} async-done(((bf16[272,1088]{1,0:T(8,128)(2,1)}), bf16[1088,1088]{1,0:T(8,128)(2,1)}) %all-gather.16.cloned.1.call-update) | async-done | bytes 2367504 | tf_op jit(solution)/shard_map/all_gather | solution.py:59
  302.5 95.1 %all-gather.18.cloned.1.call-done = bf16[1088,4352]{1,0:T(8,128)(2,1)} async-done(((bf16[272,4352]{1,0:T(8,128)(2,1)}), bf16[1088,4352]{1,0:T(8,128)(2,1)}) %all-gather.18.cloned.1.call-update) | async-done | bytes 9469968 | tf_op jit(solution)/shard_map/all_gather | solution.py:60
  397.7 9.7 fusion.50
  417.8 17.2 %all_gather.48 = f32[2,512,17]{2,0,1:T(2,128)S(1)} all-gather(f32[2,64,17]{2,0,1:T(2,128)S(1)} %copy.114), channel_id=1, replica_groups=mesh['fsdp'=4,'ctx'=8] {'ctx'}, dimensions={1}, use_global_device_ids=true | all-gather | bytes 78336 | tf_op jit(solution)/shard_map/all_gather | solution.py:165
  435.4 16.0 %all_gather.46 = f32[2,512,17]{2,0,1:T(2,128)S(1)} all-gather(f32[2,64,17]{2,0,1:T(2,128)S(1)} %copy.109), channel_id=1, replica_groups=mesh['fsdp'=4,'ctx'=8] {'ctx'}, dimensions={1}, use_global_device_ids=true | all-gather | bytes 78336 | tf_op jit(solution)/shard_map/all_gather | solution.py:164
  458.5 10.4 all-gather.24.cloned.1.call-done
  491.5 9.6 fusion.33
  501.1 11.4 fusion.49
  524.8 15.9 %reduce-scatter.8.cloned.1.call-done = f32[2,64,1088]{2,1,0:T(8,128)} async-done(((f32[2,512,1088]{2,1,0:T(8,128)}), f32[2,64,1088]{2,1,0:T(8,128)}) %reduce-scatter.8.cloned.1.call-update) | async-done | bytes 557072 | tf_op jit(solution)/shard_map/reduce_scatter | solution.py:223
  542.5 7.8 fusion.47
  550.4 51.7 %reduce-scatter.16.cloned.1.call-done = f32[272,1088]{1,0:T(8,128)} async-done(((f32[1088,1088]{1,0:T(8,128)}), f32[272,1088]{1,0:T(8,128)}) %reduce-scatter.16.cloned.1.call-update) | async-done | bytes 1183760
  602.1 175.7 %reduce-scatter.12.cloned.1.call-done = f32[272,4352]{1,0:T(8,128)} async-done(((f32[1088,4352]{1,0:T(8,128)}), f32[272,4352]{1,0:T(8,128)}) %reduce-scatter.12.cloned.1.call-update) | async-done | bytes 4734992 | tf_op jit(solution)/shard_map/reduce_scatter | solution.py:239
  777.8 183.3 %reduce-scatter.14.cloned.1.call-done = f32[1088,1088]{1,0:T(8,128)} async-done(((f32[4352,1088]{1,0:T(8,128)}), f32[1088,1088]{1,0:T(8,128)}) %reduce-scatter.14.cloned.1.call-update) | async-done | bytes 4734992 | tf_op jit(solution)/shard_map/reduce_scatter | solution.py:242
  961.1 139.3 %reduce-scatter.10.cloned.1.call-done = f32[272,3264]{1,0:T(8,128)} async-done(((f32[1088,3264]{1,0:T(8,128)}), f32[272,3264]{1,0:T(8,128)}) %reduce-scatter.10.cloned.1.call-update) | async-done | bytes 3551248 | tf_op jit(solution)/shard_map/reduce_scatter | solution.py:233
  1101.5 8.1 fusion.3
  1117.3 43.6 %all-reduce.1 = (f32[1088]{0:T(1024)}, f32[1088]{0:T(1024)}, f32[2,1088]{1,0:T(2,128)}, f32[1088]{0:T(1024)}, f32[1088]{0:T(1024)}, /*index=5*/f32[1088]{0:T(1024)}, f32[4352]{0:T(1024)}, f32[1088]{0:T(1024)}) all-reduce(f32[1088]{0:T(1024)S(1)} %get-tuple-element.69, ...), channel_id=1, replica_groups=mesh['fsdp'=4,'ctx'=8] {'fsdp','ctx'}, use_global_device_ids=true, to_apply=%region_13.14 | all-reduce | flops 13056 | bytes 104448 | tf_op jit(solution)/shard_map/psum | solution.py:248
  1160.9 237.0 %all-reduce.5.cloned.1.call-done = (f32[272,3264]{1,0:T(8,128)}, f32[272,1088]{1,0:T(8,128)}, f32[272,4352]{1,0:T(8,128)}, f32[1088,1088]{1,0:T(8,128)}) async-done(((f32[272,3264]{1,0:T(8,128)}, f32[272,1088]{1,0:T(8,128)}, f32[272,4352]{1,0:T(8,128)}, f32[1088,1088]{1,0:T(8,128)}), (f32[272,3264]{1,0:T(8,128)}, f32[272,1088]{1,0:T(8,128)}, f32[272,4352]{1,0:T(8,128)}, ...) | async-done | bytes 14204944 | tf_op jit(solution)/shard_map/psum | solution.py:245
  (203 shorter events, 98.7 us)
Async XLA Ops:
  7.2 83.3 %all-gather.10.cloned.1.call-start = ((), (), s32[]{:S(2)}) async-start(), calls=%async_computation.5 | async-start | bytes 9052160 | tf_op jit(solution)/shard_map/all_gather | solution.py:58
  7.9 82.6 %copy-start.23 = (f32[1088]{0:T(1024)S(1)}, f32[1088]{0:T(1024)}, u32[]{:S(2)}) copy-start(f32[1088]{0:T(1024)} %param.19) | copy-start | bytes 13060
  7.9 82.6 %copy-start.26 = (f32[1088]{0:T(1024)S(1)}, f32[1088]{0:T(1024)}, u32[]{:S(2)}) copy-start(f32[1088]{0:T(1024)} %param.20) | copy-start | bytes 13060
  7.9 185.6 %all-gather.20.cloned.1.call-start = ((), (), s32[]{:S(2)}) async-start(), calls=%async_computation.10 | async-start | bytes 12533760 | tf_op jit(solution)/shard_map/all_gather | solution.py:61
  8.7 218.5 %all-gather.14.cloned.1.call-start = ((), (), s32[]{:S(2)}) async-start(), calls=%async_computation.7 | async-start | bytes 2654208 | tf_op jit(solution)/shard_map/all_gather | solution.py:113
  9.1 81.4 %copy-start.34 = (f32[128]{0:T(128)}, f32[128]{0:T(128)S(1)}, u32[]{:S(2)}) copy-start(f32[128]{0:T(128)S(1)} %div.27) | copy-start | bytes 1540
  9.5 88.4 %copy-start.41 = (f32[2,1088]{1,0:T(2,128)S(1)}, f32[2,1088]{1,0:T(2,128)}, u32[]{:S(2)}) copy-start(f32[2,1088]{1,0:T(2,128)} %param.22) | copy-start | bytes 26116
  97.8 162.1 %all-gather.12.cloned.1.call-start = ((), (), s32[]{:S(2)}) async-start(), calls=%async_computation.6 | async-start | bytes 2654208 | tf_op jit(solution)/shard_map/all_gather | solution.py:114
  99.3 200.2 %all-gather.16.cloned.1.call-start = ((), (), s32[]{:S(2)}) async-start(), calls=%async_computation.8 | async-start | bytes 3133440 | tf_op jit(solution)/shard_map/all_gather | solution.py:59
  99.9 297.8 %all-gather.18.cloned.1.call-start = ((), (), s32[]{:S(2)}) async-start(), calls=%async_computation.9 | async-start | bytes 11837440 | tf_op jit(solution)/shard_map/all_gather | solution.py:60
  100.4 351.1 %all-gather.22.cloned.1.call-start = ((), (), s32[]{:S(2)}) async-start(), calls=%async_computation.11 | async-start | bytes 2654208 | tf_op jit(solution)/shard_map/all_gather | solution.py:160
  114.6 354.3 %all-gather.24.cloned.1.call-start = ((), (), s32[]{:S(2)}) async-start(), calls=%async_computation.12 | async-start | bytes 2654208 | tf_op jit(solution)/shard_map/all_gather | solution.py:161
  267.5 144.3 %copy-start.8 = (bf16[128,1088]{0,1:T(8,128)(2,1)}, bf16[128,1088]{0,1:T(8,128)(2,1)S(1)}, u32[]{:S(2)}) copy-start(bf16[128,1088]{0,1:T(8,128)(2,1)S(1)} %reshape.201) | copy-start | bytes 835588
  267.5 130.2 %copy-start.22 = (f32[1088]{0:T(1024)S(1)}, f32[1088]{0:T(1024)}, u32[]{:S(2)}) copy-start(f32[1088]{0:T(1024)} %param.25) | copy-start | bytes 13060
  267.5 130.2 %copy-start.24 = (f32[1088]{0:T(1024)S(1)}, f32[1088]{0:T(1024)}, u32[]{:S(2)}) copy-start(f32[1088]{0:T(1024)} %param.26) | copy-start | bytes 13060
  267.5 130.2 %copy-start.43 = (f32[4352]{0:T(1024)S(1)}, f32[4352]{0:T(1024)}, u32[]{:S(2)}) copy-start(f32[4352]{0:T(1024)} %param.28) | copy-start | bytes 52228
  302.3 108.4 %copy-start.32 = (f32[128]{0:T(128)}, f32[128]{0:T(128)S(1)}, u32[]{:S(2)}) copy-start(f32[128]{0:T(128)S(1)} %broadcast_multiply_fusion.6) | copy-start | bytes 1540
  302.5 108.2 %copy-start.38 = (f32[128]{0:T(128)}, f32[128]{0:T(128)S(1)}, u32[]{:S(2)}) copy-start(f32[128]{0:T(128)S(1)} %add_rsqrt_fusion.1) | copy-start | bytes 1540
  413.6 127.1 %reduce-scatter.8.cloned.1.call-start = ((), (), s32[]{:S(2)}) async-start(), calls=%async_computation.13 | async-start | bytes 5308416 | tf_op jit(solution)/shard_map/reduce_scatter | solution.py:223
  486.5 115.6 %reduce-scatter.16.cloned.1.call-start = ((), (), s32[]{:S(2)}) async-start(), calls=%async_computation.17 | async-start | bytes 6266880
  490.8 287.0 %reduce-scatter.12.cloned.1.call-start = ((), (), s32[]{:S(2)}) async-start(), calls=%async_computation.15 | async-start | bytes 23674880 | tf_op jit(solution)/shard_map/reduce_scatter | solution.py:239
  501.1 460.0 %reduce-scatter.14.cloned.1.call-start = ((), (), s32[]{:S(2)}) async-start(), calls=%async_computation.16 | async-start | bytes 25067520 | tf_op jit(solution)/shard_map/reduce_scatter | solution.py:242
  512.5 587.9 %reduce-scatter.10.cloned.1.call-start = ((), (), s32[]{:S(2)}) async-start(), calls=%async_computation.14 | async-start | bytes 18104320 | tf_op jit(solution)/shard_map/reduce_scatter | solution.py:233
  550.3 847.5 %all-reduce.5.cloned.1.call-start = ((), (), s32[]{:S(2)}) async-start(), calls=%async_computation.18 | async-start | bytes 29245440 | tf_op jit(solution)/shard_map/psum | solution.py:245
  (38 other events, 318.5 us)
Sparse Core Ops, SparseCore 0:
  9.8 80.6 all-gather.9
  92.4 101.0 all-gather.19
  195.7 31.4 all-gather.13
  229.2 30.6 all-gather.11
  261.6 37.8 all-gather.15
  301.2 96.4 all-gather.17
  399.3 35.1 all-gather.21
  436.6 32.2 all-gather.23
  486.6 54.0 reduce-scatter.7
  544.2 57.8 reduce-scatter.15
  605.2 172.5 reduce-scatter.11
  780.8 180.2 reduce-scatter.13
  964.3 136.1 reduce-scatter.9
  1103.0 294.8 all-reduce.4
where the time goes:
time: 1420 us
  waiting for transfers between devices  1160 us (82%)
  matrix products  99.5 us (7%)
  blocking collectives  88.6 us (6%)
  local copies, waits for them, and re-layouts  50.5 us (4%)
  between operations  14.8 us (1%)
    psum x1, waiting for transfers between devices, per_device(): lax.psum((joint_share, output_share, expand_share, contract_share), 'ctx')  237 us
    reduce_scatter x1, waiting for transfers between devices, per_device(): lax.psum_scatter(term_of(after_round, upper), 'fsdp', scatter_dimension=0...  183 us
    reduce_scatter x1, waiting for transfers between devices, per_device(): lax.psum_scatter(term_of(second_round, before_round), 'fsdp', scatter_dim...  176 us
    reduce_scatter x1, waiting for transfers between devices, per_device(): lax.psum_scatter(term_of(first_round, joint_grad), 'fsdp', scatter_dimens...  139 us
    all_gather x1, waiting for transfers between devices, per_device(): lax.all_gather(expand_weight, 'fsdp', axis=0, tiled=True)  95.1 us
    all_gather x1, waiting for transfers between devices, per_device(): lax.all_gather(query_key_value, 'fsdp', axis=0, tiled=True)  81.1 us
    all_gather x1, waiting for transfers between devices, per_device(): lax.all_gather(contract_weight, 'fsdp', axis=0, tiled=True)  78.9 us
    unnamed x15, waiting for transfers between devices  54.3 us
  transfers between devices with their start and end apart: 14, of which 13 were waited for; matrix products, arithmetic and copies ran while one was open for 9% of the time, Pallas kernels for 0%

commit v1 on v0

--- a/solution.py
+++ b/solution.py
@@ -1,3 +1,4 @@
+import functools
 import jax
 import jax.numpy as jnp
 from jax import lax
@@ -6,6 +7,27 @@
 HEAD_DIM = 64
 EPSILON = 1e-05
 NEGATIVE = -1e30
+
+
+def _end_core(z, at_axis):
+    val2 = lax.psum(1, "fsdp")
+    kept_arr = lax.axis_index("fsdp")
+    frame_out, e_now, current_block = (val2, kept_arr, z.shape[at_axis])
+    crops = [dd * frame_out if pp == at_axis else dd for pp, dd in enumerate(z.shape)]
+    state_next = lax.dynamic_update_slice_in_dim(
+        jnp.zeros(crops, z.dtype), z, e_now * current_block, axis=at_axis
+    )
+    for dev_j in range(1, frame_out):
+        z = lax.ppermute(
+            z, "fsdp", list(map(lambda pp: (pp, (pp + 1) % frame_out), range(frame_out)))
+        )
+        state_next = lax.dynamic_update_slice_in_dim(
+            state_next, z, (e_now - dev_j) % frame_out * current_block, axis=at_axis
+        )
+    return state_next
+
+
+watch_ticks = functools.partial(_end_core, at_axis=0)
 
 
 def layer_norm(values, gain, bias):
@@ -55,7 +77,7 @@
     scale = HEAD_DIM ** (-0.5)
     rows = sequences * piece
     joint_full, output_full, expand_full, contract_full = (
-        lax.all_gather(query_key_value, "fsdp", axis=0, tiled=True),
+        watch_ticks(query_key_value),
         lax.all_gather(output_weight, "fsdp", axis=0, tiled=True),
         lax.all_gather(expand_weight, "fsdp", axis=0, tiled=True),
         lax.all_gather(contract_weight, "fsdp", axis=0, tiled=True),

time: 1420 us -> 1550 us (1.092)
  waiting for transfers between devices: 1160 us -> 1270 us
    ppermute x0 -> x3, waiting for transfers between devices: none -> 115 us  [_end_core(): lax.ppermute(z, 'fsdp', list(map(lambda pp: (pp, (pp + 1) % frame_out), r...]
    all_gather x1, waiting for transfers between devices: 78.9 us -> 99.7 us  [per_device(): lax.all_gather(contract_weight, 'fsdp', axis=0, tiled=True)]
  transfers between devices with their start and end apart: 14 -> 17, of which waited for: 13 -> 16; matrix products, arithmetic and copies ran while one was open for 9% -> 8% of each run, Pallas kernels for 0% -> 0%
where the time goes in v1:
time: 1550 us
  waiting for transfers between devices  1270 us (82%)
  matrix products  97.2 us (6%)
  blocking collectives  90.5 us (6%)
  local copies, waits for them, and re-layouts  59.5 us (4%)
    psum x1, waiting for transfers between devices, per_device(): lax.psum((joint_share, output_share, expand_share, contract_share), 'ctx')  248 us
    reduce_scatter x1, waiting for transfers between devices, per_device(): lax.psum_scatter(term_of(after_round, upper), 'fsdp', scatter_dimension=0...  183 us
    reduce_scatter x1, waiting for transfers between devices, per_device(): lax.psum_scatter(term_of(second_round, before_round), 'fsdp', scatter_dim...  176 us
    reduce_scatter x1, waiting for transfers between devices, per_device(): lax.psum_scatter(term_of(first_round, joint_grad), 'fsdp', scatter_dimens...  139 us
    ppermute x3, waiting for transfers between devices, _end_core(): lax.ppermute(z, 'fsdp', list(map(lambda pp: (pp, (pp + 1) % frame_out), r...  115 us
    all_gather x1, waiting for transfers between devices, per_device(): lax.all_gather(contract_weight, 'fsdp', axis=0, tiled=True)  99.7 us
    all_gather x1, waiting for transfers between devices, per_device(): lax.all_gather(expand_weight, 'fsdp', axis=0, tiled=True)  90.2 us
    all_gather x1, waiting for transfers between devices, per_device(): lax.all_gather(query_key_value, 'fsdp', axis=0, tiled=True)  69.7 us
  transfers between devices with their start and end apart: 17, of which 16 were waited for; matrix products, arithmetic and copies ran while one was open for 8% of the time, Pallas kernels for 0%

profile of v1, /device:TPU:0, one launch (start us, length us, event | category | flops | bytes accessed | tf_op | source)
XLA Modules:
  0.0 1546.2 jit_solution(11512471459081106612)
XLA Ops:
  10.2 40.7 %collective-permute-done = bf16[272,3264]{1,0:T(8,128)(2,1)S(1)} collective-permute-done((bf16[272,3264]{1,0:T(8,128)(2,1)}, bf16[272,3264]{1,0:T(8,128)(2,1)S(1)}, u32[]{:S(2)}, u32[]{:S(2)}) %collective-permute-start) | collective-permute-done | bytes 1775648 | tf_op jit(solution)/shard_map/ppermute | solution.py:21
  52.8 39.8 %collective-permute-done.1 = bf16[272,3264]{1,0:T(8,128)(2,1)} collective-permute-done((bf16[272,3264]{1,0:T(8,128)(2,1)S(1)}, bf16[272,3264]{1,0:T(8,128)(2,1)}, u32[]{:S(2)}, u32[]{:S(2)}) %collective-permute-start.1) | collective-permute-done | bytes 1775648 | tf_op jit(solution)/shard_map/ppermute | solution.py:21
  98.7 34.9 %collective-permute-done.2 = bf16[272,3264]{1,0:T(8,128)(2,1)} collective-permute-done((bf16[272,3264]{1,0:T(8,128)(2,1)}, bf16[272,3264]{1,0:T(8,128)(2,1)}, u32[]{:S(2)}, u32[]{:S(2)}) %collective-permute-start.2) | collective-permute-done | bytes 1775648 | tf_op jit(solution)/shard_map/ppermute | solution.py:21
  142.9 11.8 all-gather
  157.1 14.0 all-gather.12.cloned.1.call-done
  177.2 26.8 %all-gather.10.cloned.1.call-done = bf16[2,512,1088]{2,1,0:T(8,128)(2,1)} async-done(((bf16[2,64,1088]{2,1,0:T(8,128)(2,1)}), bf16[2,512,1088]{2,1,0:T(8,128)(2,1)}) %all-gather.10.cloned.1.call-update) | async-done | bytes 2228240 | tf_op jit(solution)/shard_map/all_gather | solution.py:136
  211.3 32.4 %all-gather.14.cloned.1.call-done = bf16[1088,1088]{1,0:T(8,128)(2,1)} async-done(((bf16[272,1088]{1,0:T(8,128)(2,1)}), bf16[1088,1088]{1,0:T(8,128)(2,1)}) %all-gather.14.cloned.1.call-update) | async-done | bytes 2367504 | tf_op jit(solution)/shard_map/all_gather | solution.py:81
  246.8 99.7 %all-gather.18.cloned.1.call-done = bf16[4352,1088]{1,0:T(8,128)(2,1)} async-done(((bf16[1088,1088]{1,0:T(8,128)(2,1)}), bf16[4352,1088]{1,0:T(8,128)(2,1)}) %all-gather.18.cloned.1.call-update) | async-done | bytes 9469968 | tf_op jit(solution)/shard_map/all_gather | solution.py:83
  346.5 8.0 fusion.56
  354.5 90.2 %all-gather.16.cloned.1.call-done = bf16[1088,4352]{1,0:T(8,128)(2,1)} async-done(((bf16[272,4352]{1,0:T(8,128)(2,1)}), bf16[1088,4352]{1,0:T(8,128)(2,1)}) %all-gather.16.cloned.1.call-update) | async-done | bytes 9469968 | tf_op jit(solution)/shard_map/all_gather | solution.py:82
  444.7 9.7 fusion.50
  464.8 17.3 %all_gather.44 = f32[2,512,17]{2,0,1:T(2,128)S(1)} all-gather(f32[2,64,17]{2,0,1:T(2,128)S(1)} %copy.109), channel_id=1, replica_groups=mesh['fsdp'=4,'ctx'=8] {'ctx'}, dimensions={1}, use_global_device_ids=true | all-gather | bytes 78336 | tf_op jit(solution)/shard_map/all_gather | solution.py:186
  493.7 18.3 %all_gather.46 = f32[2,512,17]{2,0,1:T(2,128)} all-gather(f32[2,64,17]{2,0,1:T(2,128)S(1)} %copy.114), channel_id=1, replica_groups=mesh['fsdp'=4,'ctx'=8] {'ctx'}, dimensions={1}, use_global_device_ids=true | all-gather | bytes 78336 | tf_op jit(solution)/shard_map/all_gather | solution.py:187
  542.1 9.6 fusion.33
  552.2 11.4 fusion.49
  575.7 15.8 %reduce-scatter.8.cloned.1.call-done = f32[2,64,1088]{2,1,0:T(8,128)} async-done(((f32[2,512,1088]{2,1,0:T(8,128)}), f32[2,64,1088]{2,1,0:T(8,128)}) %reduce-scatter.8.cloned.1.call-update) | async-done | bytes 557072 | tf_op jit(solution)/shard_map/reduce_scatter | solution.py:245
  602.1 50.9 %reduce-scatter.16.cloned.1.call-done = f32[272,1088]{1,0:T(8,128)} async-done(((f32[1088,1088]{1,0:T(8,128)}), f32[272,1088]{1,0:T(8,128)}) %reduce-scatter.16.cloned.1.call-update) | async-done | bytes 1183760
  653.0 175.5 %reduce-scatter.12.cloned.1.call-done = f32[272,4352]{1,0:T(8,128)} async-done(((f32[1088,4352]{1,0:T(8,128)}), f32[272,4352]{1,0:T(8,128)}) %reduce-scatter.12.cloned.1.call-update) | async-done | bytes 4734992 | tf_op jit(solution)/shard_map/reduce_scatter | solution.py:261
  828.5 183.5 %reduce-scatter.14.cloned.1.call-done = f32[1088,1088]{1,0:T(8,128)} async-done(((f32[4352,1088]{1,0:T(8,128)}), f32[1088,1088]{1,0:T(8,128)}) %reduce-scatter.14.cloned.1.call-update) | async-done | bytes 4734992 | tf_op jit(solution)/shard_map/reduce_scatter | solution.py:264
  1012.0 139.2 %reduce-scatter.10.cloned.1.call-done = f32[272,3264]{1,0:T(8,128)} async-done(((f32[1088,3264]{1,0:T(8,128)}), f32[272,3264]{1,0:T(8,128)}) %reduce-scatter.10.cloned.1.call-update) | async-done | bytes 3551248 | tf_op jit(solution)/shard_map/reduce_scatter | solution.py:255
  1152.2 8.1 fusion.3
  1161.3 69.7 %all-gather.24.cloned.1.call-done = bf16[1088,3264]{1,0:T(8,128)(2,1)} async-done(((bf16[272,3264]{1,0:T(8,128)(2,1)}), bf16[1088,3264]{1,0:T(8,128)(2,1)}) %all-gather.24.cloned.1.call-update) | async-done | bytes 7102480 | tf_op jit(solution)/shard_map/all_gather | solution.py:159
  1237.7 43.1 %all-reduce.1 = (f32[1088]{0:T(1024)}, f32[1088]{0:T(1024)}, f32[2,1088]{1,0:T(2,128)}, f32[1088]{0:T(1024)}, f32[1088]{0:T(1024)}, /*index=5*/f32[1088]{0:T(1024)}, f32[4352]{0:T(1024)}, f32[1088]{0:T(1024)}) all-reduce(f32[1088]{0:T(1024)S(1)} %get-tuple-element.69, ...), channel_id=1, replica_groups=mesh['fsdp'=4,'ctx'=8] {'fsdp','ctx'}, use_global_device_ids=true, to_apply=%region_13.14 | all-reduce | flops 13056 | bytes 104448 | tf_op jit(solution)/shard_map/psum | solution.py:270
  1280.8 247.7 %all-reduce.5.cloned.1.call-done = (f32[272,3264]{1,0:T(8,128)}, f32[272,1088]{1,0:T(8,128)}, f32[272,4352]{1,0:T(8,128)}, f32[1088,1088]{1,0:T(8,128)}) async-done(((f32[272,3264]{1,0:T(8,128)}, f32[272,1088]{1,0:T(8,128)}, f32[272,4352]{1,0:T(8,128)}, f32[1088,1088]{1,0:T(8,128)}), (f32[272,3264]{1,0:T(8,128)}, f32[272,1088]{1,0:T(8,128)}, f32[272,4352]{1,0:T(8,128)}, ...) | async-done | bytes 14204944 | tf_op jit(solution)/shard_map/psum | solution.py:267
  (216 shorter events, 133.4 us)
Async XLA Ops:
  7.2 163.9 %all-gather.12.cloned.1.call-start = ((), (), s32[]{:S(2)}) async-start(), calls=%async_computation.6 | async-start | bytes 2654208 | tf_op jit(solution)/shard_map/all_gather | solution.py:135
  7.2 43.7 %collective-permute-start = (bf16[272,3264]{1,0:T(8,128)(2,1)}, bf16[272,3264]{1,0:T(8,128)(2,1)S(1)}, u32[]{:S(2)}, u32[]{:S(2)}) collective-permute-start(bf16[272,3264]{1,0:T(8,128)(2,1)} %param.21), channel_id=1, source_target_pairs={{0,8},{8,16},{16,24},{24,0},{1,9},{9,17},{17,25},{25,1},{2,10},{10... | collective-permute-start | bytes 5326856 | tf_op jit(solution)/shard_map/ppermute | solution.py:21
  50.9 41.7 %collective-permute-start.1 = (bf16[272,3264]{1,0:T(8,128)(2,1)S(1)}, bf16[272,3264]{1,0:T(8,128)(2,1)}, u32[]{:S(2)}, u32[]{:S(2)}) collective-permute-start(bf16[272,3264]{1,0:T(8,128)(2,1)S(1)} %collective-permute-done), channel_id=1, source_target_pairs={{0,8},{8,16},{16,24},{24,0},{1,9},{9,17},{17,25},{25,1},{2,10},{10... | collective-permute-start | bytes 5326856 | tf_op jit(solution)/shard_map/ppermute | solution.py:21
  92.6 41.0 %collective-permute-start.2 = (bf16[272,3264]{1,0:T(8,128)(2,1)}, bf16[272,3264]{1,0:T(8,128)(2,1)}, u32[]{:S(2)}, u32[]{:S(2)}) collective-permute-start(bf16[272,3264]{1,0:T(8,128)(2,1)} %collective-permute-done.1), channel_id=1, source_target_pairs={{0,8},{8,16},{16,24},{24,0},{1,9},{9,17},{17,25},{25,1},{2,10},{10... | collective-permute-start | bytes 5326856 | tf_op jit(solution)/shard_map/ppermute | solution.py:21
  139.5 64.4 %all-gather.10.cloned.1.call-start = ((), (), s32[]{:S(2)}) async-start(), calls=%async_computation.5 | async-start | bytes 2654208 | tf_op jit(solution)/shard_map/all_gather | solution.py:136
  140.9 102.8 %all-gather.14.cloned.1.call-start = ((), (), s32[]{:S(2)}) async-start(), calls=%async_computation.7 | async-start | bytes 3133440 | tf_op jit(solution)/shard_map/all_gather | solution.py:81
  141.7 204.8 %all-gather.18.cloned.1.call-start = ((), (), s32[]{:S(2)}) async-start(), calls=%async_computation.9 | async-start | bytes 12533760 | tf_op jit(solution)/shard_map/all_gather | solution.py:83
  142.3 302.4 %all-gather.16.cloned.1.call-start = ((), (), s32[]{:S(2)}) async-start(), calls=%async_computation.8 | async-start | bytes 11837440 | tf_op jit(solution)/shard_map/all_gather | solution.py:82
  142.9 339.4 %all-gather.20.cloned.1.call-start = ((), (), s32[]{:S(2)}) async-start(), calls=%async_computation.10 | async-start | bytes 2654208 | tf_op jit(solution)/shard_map/all_gather | solution.py:182
  157.1 362.5 %all-gather.22.cloned.1.call-start = ((), (), s32[]{:S(2)}) async-start(), calls=%async_computation.11 | async-start | bytes 2654208 | tf_op jit(solution)/shard_map/all_gather | solution.py:183
  211.2 247.6 %copy-start.9 = (bf16[128,1088]{0,1:T(8,128)(2,1)}, bf16[128,1088]{0,1:T(8,128)(2,1)S(1)}, u32[]{:S(2)}) copy-start(bf16[128,1088]{0,1:T(8,128)(2,1)S(1)} %reshape.201) | copy-start | bytes 835588
  211.3 135.3 %copy-start.13 = (bf16[2,64,1088]{2,1,0:T(8,128)(2,1)S(1)}, bf16[2,64,1088]{2,1,0:T(8,128)(2,1)}, u32[]{:S(2)}) copy-start(bf16[2,64,1088]{2,1,0:T(8,128)(2,1)} %param.31) | copy-start | bytes 835588
  246.6 211.3 %copy-start.33 = (f32[128]{0:T(128)}, f32[128]{0:T(128)S(1)}, u32[]{:S(2)}) copy-start(f32[128]{0:T(128)S(1)} %broadcast_multiply_fusion.6) | copy-start | bytes 1540
  246.7 211.1 %copy-start.39 = (f32[128]{0:T(128)}, f32[128]{0:T(128)S(1)}, u32[]{:S(2)}) copy-start(f32[128]{0:T(128)S(1)} %add_rsqrt_fusion.1) | copy-start | bytes 1540
  246.8 198.0 %copy-start.23 = (f32[1088]{0:T(1024)S(1)}, f32[1088]{0:T(1024)}, u32[]{:S(2)}) copy-start(f32[1088]{0:T(1024)} %param.25) | copy-start | bytes 13060
  246.8 198.0 %copy-start.25 = (f32[1088]{0:T(1024)S(1)}, f32[1088]{0:T(1024)}, u32[]{:S(2)}) copy-start(f32[1088]{0:T(1024)} %param.26) | copy-start | bytes 13060
  246.8 198.0 %copy-start.44 = (f32[4352]{0:T(1024)S(1)}, f32[4352]{0:T(1024)}, u32[]{:S(2)}) copy-start(f32[4352]{0:T(1024)} %param.28) | copy-start | bytes 52228
  461.4 130.0 %reduce-scatter.8.cloned.1.call-start = ((), (), s32[]{:S(2)}) async-start(), calls=%async_computation.12 | async-start | bytes 5308416 | tf_op jit(solution)/shard_map/reduce_scatter | solution.py:245
  537.1 115.8 %reduce-scatter.16.cloned.1.call-start = ((), (), s32[]{:S(2)}) async-start(), calls=%async_computation.17 | async-start | bytes 6266880
  541.5 287.1 %reduce-scatter.12.cloned.1.call-start = ((), (), s32[]{:S(2)}) async-start(), calls=%async_computation.15 | async-start | bytes 23674880 | tf_op jit(solution)/shard_map/reduce_scatter | solution.py:261
  551.7 460.3 %reduce-scatter.14.cloned.1.call-start = ((), (), s32[]{:S(2)}) async-start(), calls=%async_computation.16 | async-start | bytes 25067520 | tf_op jit(solution)/shard_map/reduce_scatter | solution.py:264
  563.6 587.6 %reduce-scatter.10.cloned.1.call-start = ((), (), s32[]{:S(2)}) async-start(), calls=%async_computation.14 | async-start | bytes 18104320 | tf_op jit(solution)/shard_map/reduce_scatter | solution.py:255
  601.1 629.9 %all-gather.24.cloned.1.call-start = ((), (), s32[]{:S(2)}) async-start(), calls=%async_computation.13 | async-start | bytes 9052160 | tf_op jit(solution)/shard_map/all_gather | solution.py:159
  601.8 926.6 %all-reduce.5.cloned.1.call-start = ((), (), s32[]{:S(2)}) async-start(), calls=%async_computation.18 | async-start | bytes 29245440 | tf_op jit(solution)/shard_map/psum | solution.py:267
  (42 other events, 454.2 us)
Sparse Core Ops, SparseCore 0:
  139.7 31.3 all-gather.11
  173.3 30.6 all-gather.9
  205.8 37.8 all-gather.13
  245.4 101.0 all-gather.17
  348.2 96.4 all-gather.15
  446.8 35.3 all-gather.19
  484.3 35.1 all-gather.21
  537.2 54.1 reduce-scatter.7
  595.1 57.8 reduce-scatter.15
  655.9 172.5 reduce-scatter.11
  831.7 180.2 reduce-scatter.13
  1015.0 136.1 reduce-scatter.9
  1153.1 77.9 all-gather.23
  1233.5 294.8 all-reduce.4
